TPU v7x, 32 devices: a whole 2x2x4 slice. The times are simulated.
32 devices in a mesh: sect: 4 (over y, x), tile: 8 (over z, core).
Axes of the slice: x: 2, y: 2, z: 4, core: 2. Of those that a mesh axis runs over, the one named last changes fastest.
Arguments:
- zonal: float32 [4, 64, 512], P('sect', 'tile'), may hold values from -1.5 to 1.5
- merid: float32 [4, 64, 512], P('sect', 'tile'), may hold values from -1.5 to 1.5
- height: float32 [4, 64, 512], P('sect', 'tile'), may hold values from -6 to 6
- level_kappa: float32 [4], replicated, may hold values from 0.2 to 2
- sea: int32 [64, 512], P('tile'), may hold values 0 or 1
- flags: int32 [4, 64, 512], P(None, 'tile', 'sect'), may hold values 0 or 1
- conc: float32 [12, 4, 64, 512], P(None, None, 'tile', 'sect'), may hold values from 0.1 to 2
- react: float32 [12, 12], replicated, may hold values from -1.2 to 1.2
- absorb: float32 [12], replicated, may hold values from 0.05 to 1
- light: float32 [4], replicated, may hold values from 0.1 to 1
Outputs:
- conc_out: float32 [12, 4, 64, 512], P(None, None, 'tile', 'sect')
- zonal_out: float32 [4, 64, 512], P('sect', 'tile')
- merid_out: float32 [4, 64, 512], P('sect', 'tile')
- height_out: float32 [4, 64, 512], P('sect', 'tile')
All inputs are finite; a program needn't handle non-finite values. No bound on the sum of `sea` or of `flags` on one device may be relied on, other than what follows from the above.
Results may differ from a plain program's by a relative error of at most 0.00022.
Values sent between devices are 32-bit elements; how exact they have to be, the bound alone decides.
A program may use at most 64 MiB of HBM per device.

v0:
```python
import jax
import jax.numpy as jnp
from jax import lax
from jax.sharding import PartitionSpec as P

STEPS = 4
INTERVALS = 2
time_step = 0.1
gravity = 1.0
coriolis = 0.3
viscosity = 0.05
heat_coupling = 0.05
tracer_step = 0.5
stir_gain = 4.0


def padded_2(cells, sides, width):
    for axis, dim in sides:
        count = lax.axis_size(axis)
        head = lax.slice_in_dim(cells, 0, width, axis=dim)
        tail = lax.slice_in_dim(cells, cells.shape[dim] - width, cells.shape[dim], axis=dim)
        cells = jnp.concatenate(
            [
                lax.ppermute(tail, axis, [(i, (i + 1) % count) for i in range(count)]),
                cells,
                lax.ppermute(head, axis, [((i + 1) % count, i) for i in range(count)]),
            ],
            axis=dim,
        )
    return cells


def along_x(field):
    return 0.5 * (jnp.roll(field, -1, 2) - jnp.roll(field, 1, 2))


def along_y(padded):
    return 0.5 * (padded[:, 2:] - padded[:, :-2])


def laplace(field, padded):
    total = padded[:, 2:] + padded[:, :-2]
    total = total + jnp.roll(field, -1, 2) + jnp.roll(field, 1, 2)
    return total - 4.0 * field


def upwind(centre, ahead, behind, speed, flag):
    upper = jnp.maximum(speed, 0.0) * (centre - behind) + jnp.minimum(speed, 0.0) * (ahead - centre)
    middle = 0.5 * speed * (ahead - behind)
    return jnp.where(flag == 1, upper, middle)


def column_solve(starred, kappa):
    levels = starred.shape[1]
    couple = [tracer_step * 0.5 * (kappa[k] + kappa[k + 1]) for k in range(levels - 1)]
    factor = []
    partial_rhs = []
    for k in range(levels):
        lower = couple[k - 1] if k > 0 else jnp.zeros_like(kappa[0])
        upper = couple[k] if k < levels - 1 else jnp.zeros_like(kappa[0])
        diagonal = 1.0 + lower + upper
        if k == 0:
            denom = diagonal
            rhs_now = starred[:, 0] / denom
        else:
            denom = diagonal + lower * factor[k - 1]
            rhs_now = (starred[:, k] + lower * partial_rhs[k - 1]) / denom
        factor.append(-upper / denom)
        partial_rhs.append(rhs_now)
    result = [None] * levels
    result[levels - 1] = partial_rhs[levels - 1]
    for k in range(levels - 2, -1, -1):
        result[k] = partial_rhs[k] - factor[k] * result[k + 1]
    return jnp.stack(result, axis=1)


def body(zonal, merid, height, level_kappa, sea, flags, conc, react, absorb, light):
    sect_index = lax.axis_index("sect")
    levels_dev = zonal.shape[0]
    column_dev = conc.shape[3]
    wet_rows = sea.astype(jnp.float32)
    wet_cols = lax.dynamic_slice_in_dim(wet_rows, sect_index * column_dev, column_dev, 1)
    own_kappa = lax.dynamic_slice_in_dim(level_kappa, sect_index * levels_dev, levels_dev, 0)
    forcing = jnp.zeros(height.shape, jnp.float32)
    for interval in range(INTERVALS):
        zonal_sum = jnp.zeros(zonal.shape, jnp.float32)
        merid_sum = jnp.zeros(merid.shape, jnp.float32)
        for step in range(STEPS):
            forced = height + time_step * heat_coupling * forcing
            wide = padded_2(jnp.stack([zonal, merid, forced]), (("tile", 2),), 2)
            zonal_wide = wide[0]
            merid_wide = wide[1]
            forced_wide = wide[2]
            zonal_pad = zonal_wide[:, 1:-1]
            merid_pad = merid_wide[:, 1:-1]
            height_ext = forced_wide[:, 1:-1] - time_step * (
                along_x(zonal_pad) + along_y(merid_wide)
            )
            height = height_ext[:, 1:-1]
            zonal_new = wet_rows * (
                zonal
                + time_step
                * (
                    coriolis * merid
                    - gravity * along_x(height)
                    + viscosity * laplace(zonal, zonal_pad)
                )
            )
            merid_new = wet_rows * (
                merid
                + time_step
                * (
                    -coriolis * zonal
                    - gravity * along_y(height_ext)
                    + viscosity * laplace(merid, merid_pad)
                )
            )
            zonal, merid = (zonal_new, merid_new)
            zonal_sum = zonal_sum + zonal
            merid_sum = merid_sum + merid
        zonal_mean = zonal_sum / STEPS
        merid_mean = merid_sum / STEPS
        kappa_rows = own_kappa[:, None, None] * (
            1.0 + stir_gain * (zonal_mean * zonal_mean + merid_mean * merid_mean)
        )
        arrived = lax.all_to_all(
            jnp.stack([zonal_mean, merid_mean, kappa_rows]),
            "sect",
            split_axis=3,
            concat_axis=1,
            tiled=True,
        )
        zonal_cols = arrived[0]
        merid_cols = arrived[1]
        kappa_cols = arrived[2]
        padded = padded_2(conc, (("tile", 2), ("sect", 3)), 1)
        east = padded[:, :, 1:-1, 2:]
        west = padded[:, :, 1:-1, :-2]
        north = padded[:, :, 2:, 1:-1]
        south = padded[:, :, :-2, 1:-1]
        moving_terms = upwind(conc, east, west, zonal_cols, flags) + upwind(
            conc, north, south, merid_cols, flags
        )
        starred = conc - tracer_step * wet_cols * moving_terms
        mixed = column_solve(starred, kappa_cols)
        growth = jnp.einsum("ij,jzyx->izyx", react, mixed, precision=lax.Precision.HIGHEST)
        conc = mixed + tracer_step * wet_cols * growth
        if interval + 1 < INTERVALS:
            heat_cols = light[:, None, None] * jnp.einsum(
                "k,kzyx->zyx", absorb, conc, precision=lax.Precision.HIGHEST
            )
            forcing = lax.all_to_all(heat_cols, "sect", split_axis=0, concat_axis=2, tiled=True)
    return (conc, zonal, merid, height)


def solution(mesh):
    placed = (
        P("sect", "tile", None),
        P("sect", "tile", None),
        P("sect", "tile", None),
        P(),
        P("tile", None),
        P(None, "tile", "sect"),
        P(None, None, "tile", "sect"),
        P(),
        P(),
        P(),
    )
    return jax.shard_map(
        body,
        mesh=mesh,
        in_specs=placed,
        out_specs=(
            P(None, None, "tile", "sect"),
            P("sect", "tile", None),
            P("sect", "tile", None),
            P("sect", "tile", None),
        ),
        check_vma=False,
    )
```

profile of v0, /device:TPU:0, one launch (start us, length us, event | category | flops | bytes accessed | tf_op | source)
XLA Modules:
  0.0 116.7 jit_solution(4213536475629891333)
XLA Ops:
  2.0 4.1 %collective-permute-start.1 = (f32[3,1,2,512]{3,2,1,0:T(2,128)S(1)}, f32[3,1,2,512]{3,2,1,0:T(2,128)S(1)}, u32[]{:S(2)}, u32[]{:S(2)}) collective-permute-start(f32[3,1,2,512]{3,2,1,0:T(2,128)S(1)} %get-tuple-element.119), channel_id=1, source_target_pairs={{1,0},{2,1},{3,2},{4,3},{5,4},{6,5},{7,6},{0,7},{9,8},{10,9},{11,1... | collective-permute-start | bytes 36872 | tf_op jit(solution)/shard_map/ppermute | solution.py:26
  7.2 3.5 %collective-permute-start.9 = (f32[12,4,1,128]{3,0,2,1:T(8,128)S(1)}, f32[12,4,1,128]{3,0,2,1:T(8,128)S(1)}, u32[]{:S(2)}, u32[]{:S(2)}) collective-permute-start(f32[12,4,1,128]{3,0,2,1:T(8,128)S(1)} %get-tuple-element.67), channel_id=1, source_target_pairs={{1,0},{2,1},{3,2},{4,3},{5,4},{6,5},{7,6},{0,7},{9,8},{10,9},{11,1... | collective-permute-start | bytes 73736 | tf_op jit(solution)/shard_map/ppermute | solution.py:26
  15.4 3.5 %collective-permute-start.3 = (f32[3,1,2,512]{3,2,1,0:T(2,128)S(1)}, f32[3,1,2,512]{3,2,1,0:T(2,128)S(1)}, u32[]{:S(2)}, u32[]{:S(2)}) collective-permute-start(f32[3,1,2,512]{3,2,1,0:T(2,128)S(1)} %get-tuple-element.117), channel_id=1, source_target_pairs={{1,0},{2,1},{3,2},{4,3},{5,4},{6,5},{7,6},{0,7},{9,8},{10,9},{11,1... | collective-permute-start | bytes 36872 | tf_op jit(solution)/shard_map/ppermute | solution.py:26
  19.0 1.3 %collective-permute-done.2 = f32[3,1,2,512]{3,2,1,0:T(2,128)S(1)} collective-permute-done((f32[3,1,2,512]{3,2,1,0:T(2,128)S(1)}, f32[3,1,2,512]{3,2,1,0:T(2,128)S(1)}, u32[]{:S(2)}, u32[]{:S(2)}) %collective-permute-start.2) | collective-permute-done | bytes 12320 | tf_op jit(solution)/shard_map/ppermute | solution.py:24
  21.2 3.6 %collective-permute-start.5 = (f32[3,1,2,512]{3,2,1,0:T(2,128)S(1)}, f32[3,1,2,512]{3,2,1,0:T(2,128)S(1)}, u32[]{:S(2)}, u32[]{:S(2)}) collective-permute-start(f32[3,1,2,512]{3,2,1,0:T(2,128)S(1)} %get-tuple-element.115), channel_id=1, source_target_pairs={{1,0},{2,1},{3,2},{4,3},{5,4},{6,5},{7,6},{0,7},{9,8},{10,9},{11,1... | collective-permute-start | bytes 36872 | tf_op jit(solution)/shard_map/ppermute | solution.py:26
  26.5 1.9 %collective-permute-start.10 = (f32[12,4,10,1]{3,0,2,1:T(8,128)}, f32[12,4,10,1]{3,0,2,1:T(8,128)S(1)}, u32[]{:S(2)}, u32[]{:S(2)}) collective-permute-start(f32[12,4,10,1]{3,0,2,1:T(8,128)} %get-tuple-element.62), channel_id=1, source_target_pairs={{0,8},{8,16},{16,24},{24,0},{1,9},{9,17},{17,25},{25,1},{2,10},{10... | collective-permute-start | bytes 5768 | tf_op jit(solution)/shard_map/ppermute | solution.py:24
  30.2 3.5 %collective-permute-start.7 = (f32[3,1,2,512]{3,2,1,0:T(2,128)S(1)}, f32[3,1,2,512]{3,2,1,0:T(2,128)S(1)}, u32[]{:S(2)}, u32[]{:S(2)}) collective-permute-start(f32[3,1,2,512]{3,2,1,0:T(2,128)S(1)} %get-tuple-element.113), channel_id=1, source_target_pairs={{1,0},{2,1},{3,2},{4,3},{5,4},{6,5},{7,6},{0,7},{9,8},{10,9},{11,1... | collective-permute-start | bytes 36872 | tf_op jit(solution)/shard_map/ppermute | solution.py:26
  37.8 3.3 %reduce = f32[512,3,8]{2,1,0:T(4,128)S(1)} reduce(f32[512,3,1,8]{3,2,1,0:T(1,128)S(1)} %bitcast.205, f32[]{:T(128)} %broadcast.650), dimensions={2}, to_apply=%bitcast.189.reduce_sub_computation | reduce | bytes 98308
  42.4 3.3 %all-to-all-start = ((f32[4,1,3072]{2,1,0:T(1,128)}), f32[4,1,3072]{2,1,0:T(1,128)S(1)}, u32[]{:S(2)}, u32[]{:S(2)}) async-start(f32[4,1,3072]{2,1,0:T(1,128)} %reshape.1284), calls=%async_computation | async-start | bytes 98304 | tf_op jit(solution)/shard_map/all_to_all | solution.py:126
  45.9 4.6 %all-to-all-done = f32[4,1,3072]{2,1,0:T(1,128)S(1)} async-done(((f32[4,1,3072]{2,1,0:T(1,128)}), f32[4,1,3072]{2,1,0:T(1,128)S(1)}, u32[]{:S(2)}, u32[]{:S(2)}) %all-to-all-start) | async-done | bytes 49184 | tf_op jit(solution)/shard_map/all_to_all | solution.py:126
  56.9 3.3 %all-to-all-start.1 = ((f32[4,8,128]{2,1,0:T(8,128)}), f32[4,8,128]{2,1,0:T(8,128)S(1)}, u32[]{:S(2)}, u32[]{:S(2)}) async-start(f32[4,8,128]{2,1,0:T(8,128)} %broadcast_multiply_fusion), calls=%async_computation.1 | async-start | bytes 32768 | tf_op jit(solution)/shard_map/all_to_all | solution.py:152
  60.2 4.6 %all-to-all-done.1 = f32[4,8,128]{2,1,0:T(8,128)S(1)} async-done(((f32[4,8,128]{2,1,0:T(8,128)}), f32[4,8,128]{2,1,0:T(8,128)S(1)}, u32[]{:S(2)}, u32[]{:S(2)}) %all-to-all-start.1) | async-done | bytes 16416 | tf_op jit(solution)/shard_map/all_to_all | solution.py:152
  64.9 3.5 %collective-permute-start.13 = (f32[3,1,2,512]{3,2,1,0:T(2,128)S(1)}, f32[3,1,2,512]{3,2,1,0:T(2,128)S(1)}, u32[]{:S(2)}, u32[]{:S(2)}) collective-permute-start(f32[3,1,2,512]{3,2,1,0:T(2,128)S(1)} %get-tuple-element.105), channel_id=1, source_target_pairs={{1,0},{2,1},{3,2},{4,3},{5,4},{6,5},{7,6},{0,7},{9,8},{10,9},{11,1... | collective-permute-start | bytes 36872 | tf_op jit(solution)/shard_map/ppermute | solution.py:26
  68.5 3.5 %collective-permute-start.21 = (f32[12,4,1,128]{3,0,2,1:T(8,128)S(1)}, f32[12,4,1,128]{3,0,2,1:T(8,128)S(1)}, u32[]{:S(2)}, u32[]{:S(2)}) collective-permute-start(f32[12,4,1,128]{3,0,2,1:T(8,128)S(1)} %get-tuple-element.65), channel_id=1, source_target_pairs={{1,0},{2,1},{3,2},{4,3},{5,4},{6,5},{7,6},{0,7},{9,8},{10,9},{11,1... | collective-permute-start | bytes 73736 | tf_op jit(solution)/shard_map/ppermute | solution.py:26
  73.0 3.5 %collective-permute-start.15 = (f32[3,1,2,512]{3,2,1,0:T(2,128)S(1)}, f32[3,1,2,512]{3,2,1,0:T(2,128)S(1)}, u32[]{:S(2)}, u32[]{:S(2)}) collective-permute-start(f32[3,1,2,512]{3,2,1,0:T(2,128)S(1)} %get-tuple-element.103), channel_id=1, source_target_pairs={{1,0},{2,1},{3,2},{4,3},{5,4},{6,5},{7,6},{0,7},{9,8},{10,9},{11,1... | collective-permute-start | bytes 36872 | tf_op jit(solution)/shard_map/ppermute | solution.py:26
  76.6 1.3 %collective-permute-done.14 = f32[3,1,2,512]{3,2,1,0:T(2,128)S(1)} collective-permute-done((f32[3,1,2,512]{3,2,1,0:T(2,128)S(1)}, f32[3,1,2,512]{3,2,1,0:T(2,128)S(1)}, u32[]{:S(2)}, u32[]{:S(2)}) %collective-permute-start.14) | collective-permute-done | bytes 12320 | tf_op jit(solution)/shard_map/ppermute | solution.py:24
  78.8 3.6 %collective-permute-start.17 = (f32[3,1,2,512]{3,2,1,0:T(2,128)S(1)}, f32[3,1,2,512]{3,2,1,0:T(2,128)S(1)}, u32[]{:S(2)}, u32[]{:S(2)}) collective-permute-start(f32[3,1,2,512]{3,2,1,0:T(2,128)S(1)} %get-tuple-element.101), channel_id=1, source_target_pairs={{1,0},{2,1},{3,2},{4,3},{5,4},{6,5},{7,6},{0,7},{9,8},{10,9},{11,1... | collective-permute-start | bytes 36872 | tf_op jit(solution)/shard_map/ppermute | solution.py:26
  84.7 3.7 %collective-permute-start.19 = (f32[3,1,2,512]{3,2,1,0:T(2,128)S(1)}, f32[3,1,2,512]{3,2,1,0:T(2,128)S(1)}, u32[]{:S(2)}, u32[]{:S(2)}) collective-permute-start(f32[3,1,2,512]{3,2,1,0:T(2,128)S(1)} %get-tuple-element.99), channel_id=1, source_target_pairs={{1,0},{2,1},{3,2},{4,3},{5,4},{6,5},{7,6},{0,7},{9,8},{10,9},{11,1... | collective-permute-start | bytes 36872 | tf_op jit(solution)/shard_map/ppermute | solution.py:26
  90.3 1.4 %multiply_bitcast_fusion.2 = (f32[1,1,8,512]{3,2,1,0:T(8,128)S(1)}, f32[1,8,512]{2,1,0:T(8,128)S(1)}, f32[1,8,512]{2,1,0:T(8,128)}, f32[1,8,512]{2,1,0:T(8,128)S(1)}, f32[1,8,512]{2,1,0:T(8,128)}) fusion(f32[]{:T(128)} %bitcast.27, f32[1,8,512]{2,1,0:T(8,128)S(1)} %fusion.106, f32[1,8,512]{2,1,0:T(8,128)S(1)} %fusion.144, f32[1,8,512]{2,1,0:T(8,128)S(1)} %fusion.125, ...), kind=kLoop, calls=%fused_computation.359 | loop fusion | flops 200704 | bytes 393220 | tf_op jit(solution)/shard_map/stack | solution.py:127
  92.6 3.3 %reduce.2 = f32[512,3,8]{2,1,0:T(4,128)S(1)} reduce(f32[512,3,1,8]{3,2,1,0:T(1,128)S(1)} %bitcast.207, f32[]{:T(128)} %broadcast.650), dimensions={2}, to_apply=%bitcast.191.reduce_sub_computation | reduce | bytes 98308
  97.2 3.3 %all-to-all-start.2 = ((f32[4,1,3072]{2,1,0:T(1,128)}), f32[4,1,3072]{2,1,0:T(1,128)S(1)}, u32[]{:S(2)}, u32[]{:S(2)}) async-start(f32[4,1,3072]{2,1,0:T(1,128)} %reshape.1286), calls=%async_computation.2 | async-start | bytes 98304 | tf_op jit(solution)/shard_map/all_to_all | solution.py:126
  100.6 2.0 %collective-permute-start.22 = (f32[12,4,10,1]{3,0,2,1:T(8,128)S(1)}, f32[12,4,10,1]{3,0,2,1:T(8,128)S(1)}, u32[]{:S(2)}, u32[]{:S(2)}) collective-permute-start(f32[12,4,10,1]{3,0,2,1:T(8,128)S(1)} %get-tuple-element.60), channel_id=1, source_target_pairs={{0,8},{8,16},{16,24},{24,0},{1,9},{9,17},{17,25},{25,1},{2,10},{10... | collective-permute-start | bytes 5768 | tf_op jit(solution)/shard_map/ppermute | solution.py:24
  108.3 3.3 %collective-permute-done.22 = f32[12,4,10,1]{3,0,2,1:T(8,128)S(1)} collective-permute-done((f32[12,4,10,1]{3,0,2,1:T(8,128)S(1)}, f32[12,4,10,1]{3,0,2,1:T(8,128)S(1)}, u32[]{:S(2)}, u32[]{:S(2)}) %collective-permute-start.22) | collective-permute-done | bytes 1952 | tf_op jit(solution)/shard_map/ppermute | solution.py:24
  111.6 3.6 %collective-permute-done.23 = f32[12,4,10,1]{3,0,2,1:T(8,128)S(1)} collective-permute-done((f32[12,4,10,1]{3,0,2,1:T(8,128)S(1)}, f32[12,4,10,1]{3,0,2,1:T(8,128)S(1)}, u32[]{:S(2)}, u32[]{:S(2)}) %collective-permute-start.23) | collective-permute-done | bytes 1952 | tf_op jit(solution)/shard_map/ppermute | solution.py:26
  (211 shorter events, 38.8 us)
Async XLA Ops:
  1.5 13.0 %collective-permute-start = (f32[3,1,2,512]{3,2,1,0:T(2,128)S(1)}, f32[3,1,2,512]{3,2,1,0:T(2,128)S(1)}, u32[]{:S(2)}, u32[]{:S(2)}) collective-permute-start(f32[3,1,2,512]{3,2,1,0:T(2,128)S(1)} %get-tuple-element.118), channel_id=1, source_target_pairs={{0,1},{1,2},{2,3},{3,4},{4,5},{5,6},{6,7},{7,0},{8,9},{9,10},{10,1... | collective-permute-start | bytes 36872 | tf_op jit(solution)/shard_map/ppermute | solution.py:24
  2.0 12.4 %collective-permute-start.1 = (f32[3,1,2,512]{3,2,1,0:T(2,128)S(1)}, f32[3,1,2,512]{3,2,1,0:T(2,128)S(1)}, u32[]{:S(2)}, u32[]{:S(2)}) collective-permute-start(f32[3,1,2,512]{3,2,1,0:T(2,128)S(1)} %get-tuple-element.119), channel_id=1, source_target_pairs={{1,0},{2,1},{3,2},{4,3},{5,4},{6,5},{7,6},{0,7},{9,8},{10,9},{11,1... | collective-permute-start | bytes 36872 | tf_op jit(solution)/shard_map/ppermute | solution.py:26
  7.2 17.6 %collective-permute-start.8 = (f32[12,4,1,128]{3,0,2,1:T(8,128)S(1)}, f32[12,4,1,128]{3,0,2,1:T(8,128)S(1)}, u32[]{:S(2)}, u32[]{:S(2)}) collective-permute-start(f32[12,4,1,128]{3,0,2,1:T(8,128)S(1)} %get-tuple-element.66), channel_id=1, source_target_pairs={{0,1},{1,2},{2,3},{3,4},{4,5},{5,6},{6,7},{7,0},{8,9},{9,10},{10,1... | collective-permute-start | bytes 73736 | tf_op jit(solution)/shard_map/ppermute | solution.py:24
  7.2 17.7 %collective-permute-start.9 = (f32[12,4,1,128]{3,0,2,1:T(8,128)S(1)}, f32[12,4,1,128]{3,0,2,1:T(8,128)S(1)}, u32[]{:S(2)}, u32[]{:S(2)}) collective-permute-start(f32[12,4,1,128]{3,0,2,1:T(8,128)S(1)} %get-tuple-element.67), channel_id=1, source_target_pairs={{1,0},{2,1},{3,2},{4,3},{5,4},{6,5},{7,6},{0,7},{9,8},{10,9},{11,1... | collective-permute-start | bytes 73736 | tf_op jit(solution)/shard_map/ppermute | solution.py:26
  15.3 5.0 %collective-permute-start.2 = (f32[3,1,2,512]{3,2,1,0:T(2,128)S(1)}, f32[3,1,2,512]{3,2,1,0:T(2,128)S(1)}, u32[]{:S(2)}, u32[]{:S(2)}) collective-permute-start(f32[3,1,2,512]{3,2,1,0:T(2,128)S(1)} %get-tuple-element.116), channel_id=1, source_target_pairs={{0,1},{1,2},{2,3},{3,4},{4,5},{5,6},{6,7},{7,0},{8,9},{9,10},{10,1... | collective-permute-start | bytes 36872 | tf_op jit(solution)/shard_map/ppermute | solution.py:24
  21.2 8.3 %collective-permute-start.4 = (f32[3,1,2,512]{3,2,1,0:T(2,128)S(1)}, f32[3,1,2,512]{3,2,1,0:T(2,128)S(1)}, u32[]{:S(2)}, u32[]{:S(2)}) collective-permute-start(f32[3,1,2,512]{3,2,1,0:T(2,128)S(1)} %get-tuple-element.114), channel_id=1, source_target_pairs={{0,1},{1,2},{2,3},{3,4},{4,5},{5,6},{6,7},{7,0},{8,9},{9,10},{10,1... | collective-permute-start | bytes 36872 | tf_op jit(solution)/shard_map/ppermute | solution.py:24
  21.2 8.2 %collective-permute-start.5 = (f32[3,1,2,512]{3,2,1,0:T(2,128)S(1)}, f32[3,1,2,512]{3,2,1,0:T(2,128)S(1)}, u32[]{:S(2)}, u32[]{:S(2)}) collective-permute-start(f32[3,1,2,512]{3,2,1,0:T(2,128)S(1)} %get-tuple-element.115), channel_id=1, source_target_pairs={{1,0},{2,1},{3,2},{4,3},{5,4},{6,5},{7,6},{0,7},{9,8},{10,9},{11,1... | collective-permute-start | bytes 36872 | tf_op jit(solution)/shard_map/ppermute | solution.py:26
  26.5 26.9 %collective-permute-start.10 = (f32[12,4,10,1]{3,0,2,1:T(8,128)}, f32[12,4,10,1]{3,0,2,1:T(8,128)S(1)}, u32[]{:S(2)}, u32[]{:S(2)}) collective-permute-start(f32[12,4,10,1]{3,0,2,1:T(8,128)} %get-tuple-element.62), channel_id=1, source_target_pairs={{0,8},{8,16},{16,24},{24,0},{1,9},{9,17},{17,25},{25,1},{2,10},{10... | collective-permute-start | bytes 5768 | tf_op jit(solution)/shard_map/ppermute | solution.py:24
  28.5 25.0 %collective-permute-start.11 = (f32[12,4,10,1]{3,0,2,1:T(8,128)S(1)}, f32[12,4,10,1]{3,0,2,1:T(8,128)S(1)}, u32[]{:S(2)}, u32[]{:S(2)}) collective-permute-start(f32[12,4,10,1]{3,0,2,1:T(8,128)S(1)} %get-tuple-element.63), channel_id=1, source_target_pairs={{8,0},{16,8},{24,16},{0,24},{9,1},{17,9},{25,17},{1,25},{10,2},{18... | collective-permute-start | bytes 5768 | tf_op jit(solution)/shard_map/ppermute | solution.py:26
  30.2 5.0 %collective-permute-start.6 = (f32[3,1,2,512]{3,2,1,0:T(2,128)S(1)}, f32[3,1,2,512]{3,2,1,0:T(2,128)S(1)}, u32[]{:S(2)}, u32[]{:S(2)}) collective-permute-start(f32[3,1,2,512]{3,2,1,0:T(2,128)S(1)} %get-tuple-element.112), channel_id=1, source_target_pairs={{0,1},{1,2},{2,3},{3,4},{4,5},{5,6},{6,7},{7,0},{8,9},{9,10},{10,1... | collective-permute-start | bytes 36872 | tf_op jit(solution)/shard_map/ppermute | solution.py:24
  42.4 8.1 %all-to-all-start = ((f32[4,1,3072]{2,1,0:T(1,128)}), f32[4,1,3072]{2,1,0:T(1,128)S(1)}, u32[]{:S(2)}, u32[]{:S(2)}) async-start(f32[4,1,3072]{2,1,0:T(1,128)} %reshape.1284), calls=%async_computation | async-start | bytes 98304 | tf_op jit(solution)/shard_map/all_to_all | solution.py:126
  56.9 7.9 %all-to-all-start.1 = ((f32[4,8,128]{2,1,0:T(8,128)}), f32[4,8,128]{2,1,0:T(8,128)S(1)}, u32[]{:S(2)}, u32[]{:S(2)}) async-start(f32[4,8,128]{2,1,0:T(8,128)} %broadcast_multiply_fusion), calls=%async_computation.1 | async-start | bytes 32768 | tf_op jit(solution)/shard_map/all_to_all | solution.py:152
  64.8 7.2 %collective-permute-start.12 = (f32[3,1,2,512]{3,2,1,0:T(2,128)S(1)}, f32[3,1,2,512]{3,2,1,0:T(2,128)S(1)}, u32[]{:S(2)}, u32[]{:S(2)}) collective-permute-start(f32[3,1,2,512]{3,2,1,0:T(2,128)S(1)} %get-tuple-element.104), channel_id=1, source_target_pairs={{0,1},{1,2},{2,3},{3,4},{4,5},{5,6},{6,7},{7,0},{8,9},{9,10},{10,1... | collective-permute-start | bytes 36872 | tf_op jit(solution)/shard_map/ppermute | solution.py:24
  64.9 7.1 %collective-permute-start.13 = (f32[3,1,2,512]{3,2,1,0:T(2,128)S(1)}, f32[3,1,2,512]{3,2,1,0:T(2,128)S(1)}, u32[]{:S(2)}, u32[]{:S(2)}) collective-permute-start(f32[3,1,2,512]{3,2,1,0:T(2,128)S(1)} %get-tuple-element.105), channel_id=1, source_target_pairs={{1,0},{2,1},{3,2},{4,3},{5,4},{6,5},{7,6},{0,7},{9,8},{10,9},{11,1... | collective-permute-start | bytes 36872 | tf_op jit(solution)/shard_map/ppermute | solution.py:26
  68.5 8.1 %collective-permute-start.20 = (f32[12,4,1,128]{3,0,2,1:T(8,128)S(1)}, f32[12,4,1,128]{3,0,2,1:T(8,128)S(1)}, u32[]{:S(2)}, u32[]{:S(2)}) collective-permute-start(f32[12,4,1,128]{3,0,2,1:T(8,128)S(1)} %get-tuple-element.64), channel_id=1, source_target_pairs={{0,1},{1,2},{2,3},{3,4},{4,5},{5,6},{6,7},{7,0},{8,9},{9,10},{10,1... | collective-permute-start | bytes 73736 | tf_op jit(solution)/shard_map/ppermute | solution.py:24
  68.5 8.1 %collective-permute-start.21 = (f32[12,4,1,128]{3,0,2,1:T(8,128)S(1)}, f32[12,4,1,128]{3,0,2,1:T(8,128)S(1)}, u32[]{:S(2)}, u32[]{:S(2)}) collective-permute-start(f32[12,4,1,128]{3,0,2,1:T(8,128)S(1)} %get-tuple-element.65), channel_id=1, source_target_pairs={{1,0},{2,1},{3,2},{4,3},{5,4},{6,5},{7,6},{0,7},{9,8},{10,9},{11,1... | collective-permute-start | bytes 73736 | tf_op jit(solution)/shard_map/ppermute | solution.py:26
  72.9 5.0 %collective-permute-start.14 = (f32[3,1,2,512]{3,2,1,0:T(2,128)S(1)}, f32[3,1,2,512]{3,2,1,0:T(2,128)S(1)}, u32[]{:S(2)}, u32[]{:S(2)}) collective-permute-start(f32[3,1,2,512]{3,2,1,0:T(2,128)S(1)} %get-tuple-element.102), channel_id=1, source_target_pairs={{0,1},{1,2},{2,3},{3,4},{4,5},{5,6},{6,7},{7,0},{8,9},{9,10},{10,1... | collective-permute-start | bytes 36872 | tf_op jit(solution)/shard_map/ppermute | solution.py:24
  78.8 5.0 %collective-permute-start.16 = (f32[3,1,2,512]{3,2,1,0:T(2,128)S(1)}, f32[3,1,2,512]{3,2,1,0:T(2,128)S(1)}, u32[]{:S(2)}, u32[]{:S(2)}) collective-permute-start(f32[3,1,2,512]{3,2,1,0:T(2,128)S(1)} %get-tuple-element.100), channel_id=1, source_target_pairs={{0,1},{1,2},{2,3},{3,4},{4,5},{5,6},{6,7},{7,0},{8,9},{9,10},{10,1... | collective-permute-start | bytes 36872 | tf_op jit(solution)/shard_map/ppermute | solution.py:24
  78.8 5.0 %collective-permute-start.17 = (f32[3,1,2,512]{3,2,1,0:T(2,128)S(1)}, f32[3,1,2,512]{3,2,1,0:T(2,128)S(1)}, u32[]{:S(2)}, u32[]{:S(2)}) collective-permute-start(f32[3,1,2,512]{3,2,1,0:T(2,128)S(1)} %get-tuple-element.101), channel_id=1, source_target_pairs={{1,0},{2,1},{3,2},{4,3},{5,4},{6,5},{7,6},{0,7},{9,8},{10,9},{11,1... | collective-permute-start | bytes 36872 | tf_op jit(solution)/shard_map/ppermute | solution.py:26
  84.7 5.0 %collective-permute-start.18 = (f32[3,1,2,512]{3,2,1,0:T(2,128)S(1)}, f32[3,1,2,512]{3,2,1,0:T(2,128)S(1)}, u32[]{:S(2)}, u32[]{:S(2)}) collective-permute-start(f32[3,1,2,512]{3,2,1,0:T(2,128)S(1)} %get-tuple-element.98), channel_id=1, source_target_pairs={{0,1},{1,2},{2,3},{3,4},{4,5},{5,6},{6,7},{7,0},{8,9},{9,10},{10,1... | collective-permute-start | bytes 36872 | tf_op jit(solution)/shard_map/ppermute | solution.py:24
  84.7 5.2 %collective-permute-start.19 = (f32[3,1,2,512]{3,2,1,0:T(2,128)S(1)}, f32[3,1,2,512]{3,2,1,0:T(2,128)S(1)}, u32[]{:S(2)}, u32[]{:S(2)}) collective-permute-start(f32[3,1,2,512]{3,2,1,0:T(2,128)S(1)} %get-tuple-element.99), channel_id=1, source_target_pairs={{1,0},{2,1},{3,2},{4,3},{5,4},{6,5},{7,6},{0,7},{9,8},{10,9},{11,1... | collective-permute-start | bytes 36872 | tf_op jit(solution)/shard_map/ppermute | solution.py:26
  97.2 8.2 %all-to-all-start.2 = ((f32[4,1,3072]{2,1,0:T(1,128)}), f32[4,1,3072]{2,1,0:T(1,128)S(1)}, u32[]{:S(2)}, u32[]{:S(2)}) async-start(f32[4,1,3072]{2,1,0:T(1,128)} %reshape.1286), calls=%async_computation.2 | async-start | bytes 98304 | tf_op jit(solution)/shard_map/all_to_all | solution.py:126
  100.6 11.0 %collective-permute-start.22 = (f32[12,4,10,1]{3,0,2,1:T(8,128)S(1)}, f32[12,4,10,1]{3,0,2,1:T(8,128)S(1)}, u32[]{:S(2)}, u32[]{:S(2)}) collective-permute-start(f32[12,4,10,1]{3,0,2,1:T(8,128)S(1)} %get-tuple-element.60), channel_id=1, source_target_pairs={{0,8},{8,16},{16,24},{24,0},{1,9},{9,17},{17,25},{25,1},{2,10},{10... | collective-permute-start | bytes 5768 | tf_op jit(solution)/shard_map/ppermute | solution.py:24
  102.6 12.5 %collective-permute-start.23 = (f32[12,4,10,1]{3,0,2,1:T(8,128)S(1)}, f32[12,4,10,1]{3,0,2,1:T(8,128)S(1)}, u32[]{:S(2)}, u32[]{:S(2)}) collective-permute-start(f32[12,4,10,1]{3,0,2,1:T(8,128)S(1)} %get-tuple-element.61), channel_id=1, source_target_pairs={{8,0},{16,8},{24,16},{0,24},{9,1},{17,9},{25,17},{1,25},{10,2},{18... | collective-permute-start | bytes 5768 | tf_op jit(solution)/shard_map/ppermute | solution.py:26
  (15 other events, 83.1 us)
where the time goes:
time: 118 us; the launch traced here: 117 us
  starting transfers between devices  52.9 us (45%)
  waiting for transfers between devices  23.8 us (20%)
  local copies, waits for them, and re-layouts  22.7 us (19%)
  other arithmetic  14.9 us (13%)
  between operations  1.32 us (1%)
    ppermute x12, starting transfers between devices, padded_2(): lax.ppermute(head, axis, [((i + 1) % count, i) for i in range(count)])  38.1 us
    unnamed x33, local copies, waits for them, and re-layouts  12.3 us
    ppermute x12, waiting for transfers between devices, padded_2(): lax.ppermute(tail, axis, [(i, (i + 1) % count) for i in range(count)])  9.59 us
    unnamed x2, other arithmetic  6.67 us
    all_to_all x2, starting transfers between devices, body(): lax.all_to_all(jnp.stack([zonal_mean, merid_mean, kappa_rows]), 'sect', s...  6.55 us
    all_to_all x2, waiting for transfers between devices, body(): lax.all_to_all(jnp.stack([zonal_mean, merid_mean, kappa_rows]), 'sect', s...  5.67 us
    ppermute x12, starting transfers between devices, padded_2(): lax.ppermute(tail, axis, [(i, (i + 1) % count) for i in range(count)])  4.97 us
    all_to_all x1, waiting for transfers between devices, body(): lax.all_to_all(heat_cols, 'sect', split_axis=0, concat_axis=2, tiled=True)  4.61 us
  transfers between devices with their start and end apart: 27, of which 12 were waited for; matrix products, arithmetic and copies ran while one was open for 18% of the time, Pallas kernels for 0%

commit v1 on v0

--- a/solution.py
+++ b/solution.py
@@ -2,6 +2,7 @@
 import jax.numpy as jnp
 from jax import lax
 from jax.sharding import PartitionSpec as P
+from jax.lax import axis_index, axis_size, ppermute
 
 STEPS = 4
 INTERVALS = 2
@@ -149,7 +150,26 @@
             heat_cols = light[:, None, None] * jnp.einsum(
                 "k,kzyx->zyx", absorb, conc, precision=lax.Precision.HIGHEST
             )
-            forcing = lax.all_to_all(heat_cols, "sect", split_axis=0, concat_axis=2, tiled=True)
+            o_now = axis_size("sect")
+            w1, next_value = (o_now, axis_index("sect"))
+            plain = list(heat_cols.shape)
+            opened = heat_cols.shape[0] // w1
+            plain[0] = opened
+            v_next = plain[2]
+            plain[2] = v_next * w1
+            forcing = jnp.zeros(plain, heat_cols.dtype)
+            for m in [*range(w1)]:
+                built = lax.dynamic_slice_in_dim(
+                    heat_cols, (next_value ^ m) * opened, opened, axis=0
+                )
+                if m:
+                    column = []
+                    for no in tuple(range(w1)):
+                        column.append((no, no ^ m))
+                    built = ppermute(built, "sect", column)
+                forcing = lax.dynamic_update_slice_in_dim(
+                    forcing, built, (next_value ^ m) * v_next, axis=2
+                )
     return (conc, zonal, merid, height)
 
 

time: 118 us -> 115 us (0.975)
  waiting for transfers between devices: 23.8 us -> 21.1 us
    all_to_all x1 -> x0, waiting for transfers between devices: 4.61 us -> none  [body(): lax.all_to_all(heat_cols, 'sect', split_axis=0, concat_axis=2, tiled=True)]
    ppermute x0 -> x3, starting transfers between devices: none -> 3.55 us  [body(): built = ppermute(built, 'sect', column)]
    all_to_all x1 -> x0, starting transfers between devices: 3.25 us -> none  [body(): lax.all_to_all(heat_cols, 'sect', split_axis=0, concat_axis=2, tiled=True)]
    ppermute x0 -> x3, waiting for transfers between devices: none -> 2.14 us  [body(): built = ppermute(built, 'sect', column)]
  transfers between devices with their start and end apart: 27 -> 29, of which waited for: 12 -> 13; matrix products, arithmetic and copies ran while one was open for 18% -> 18% of each run, Pallas kernels for 0% -> 0%
where the time goes in v1:
time: 115 us; the launch traced here: 114 us
  starting transfers between devices  53.6 us (47%)
  local copies, waits for them, and re-layouts  22.6 us (20%)
  waiting for transfers between devices  21.1 us (18%)
  other arithmetic  14.2 us (12%)
  between operations  1.35 us (1%)
    ppermute x12, starting transfers between devices, padded_2(): lax.ppermute(head, axis, [((i + 1) % count, i) for i in range(count)])  38.1 us
    unnamed x33, local copies, waits for them, and re-layouts  12.3 us
    ppermute x12, waiting for transfers between devices, padded_2(): lax.ppermute(tail, axis, [(i, (i + 1) % count) for i in range(count)])  9.31 us
    all_to_all x2, starting transfers between devices, body(): lax.all_to_all(jnp.stack([zonal_mean, merid_mean, kappa_rows]), 'sect', s...  6.9 us
    unnamed x2, other arithmetic  6.67 us
    all_to_all x2, waiting for transfers between devices, body(): lax.all_to_all(jnp.stack([zonal_mean, merid_mean, kappa_rows]), 'sect', s...  5.67 us
    ppermute x12, starting transfers between devices, padded_2(): lax.ppermute(tail, axis, [(i, (i + 1) % count) for i in range(count)])  5.01 us
    ppermute x12, waiting for transfers between devices, padded_2(): lax.ppermute(head, axis, [((i + 1) % count, i) for i in range(count)])  3.96 us
  transfers between devices with their start and end apart: 29, of which 13 were waited for; matrix products, arithmetic and copies ran while one was open for 18% of the time, Pallas kernels for 0%

profile of v1, /device:TPU:0, one launch (start us, length us, event | category | flops | bytes accessed | tf_op | source)
XLA Modules:
  0.0 113.9 jit_solution(9125977224039735840)
XLA Ops:
  2.0 4.1 %collective-permute-start.1 = (f32[3,1,2,512]{3,2,1,0:T(2,128)S(1)}, f32[3,1,2,512]{3,2,1,0:T(2,128)S(1)}, u32[]{:S(2)}, u32[]{:S(2)}) collective-permute-start(f32[3,1,2,512]{3,2,1,0:T(2,128)S(1)} %get-tuple-element.119), channel_id=1, source_target_pairs={{1,0},{2,1},{3,2},{4,3},{5,4},{6,5},{7,6},{0,7},{9,8},{10,9},{11,1... | collective-permute-start | bytes 36872 | tf_op jit(solution)/shard_map/ppermute | solution.py:27
  7.2 3.5 %collective-permute-start.9 = (f32[12,4,1,128]{3,0,2,1:T(8,128)S(1)}, f32[12,4,1,128]{3,0,2,1:T(8,128)S(1)}, u32[]{:S(2)}, u32[]{:S(2)}) collective-permute-start(f32[12,4,1,128]{3,0,2,1:T(8,128)S(1)} %get-tuple-element.67), channel_id=1, source_target_pairs={{1,0},{2,1},{3,2},{4,3},{5,4},{6,5},{7,6},{0,7},{9,8},{10,9},{11,1... | collective-permute-start | bytes 73736 | tf_op jit(solution)/shard_map/ppermute | solution.py:27
  15.3 3.5 %collective-permute-start.3 = (f32[3,1,2,512]{3,2,1,0:T(2,128)S(1)}, f32[3,1,2,512]{3,2,1,0:T(2,128)S(1)}, u32[]{:S(2)}, u32[]{:S(2)}) collective-permute-start(f32[3,1,2,512]{3,2,1,0:T(2,128)S(1)} %get-tuple-element.117), channel_id=1, source_target_pairs={{1,0},{2,1},{3,2},{4,3},{5,4},{6,5},{7,6},{0,7},{9,8},{10,9},{11,1... | collective-permute-start | bytes 36872 | tf_op jit(solution)/shard_map/ppermute | solution.py:27
  18.9 1.3 %collective-permute-done.2 = f32[3,1,2,512]{3,2,1,0:T(2,128)S(1)} collective-permute-done((f32[3,1,2,512]{3,2,1,0:T(2,128)S(1)}, f32[3,1,2,512]{3,2,1,0:T(2,128)S(1)}, u32[]{:S(2)}, u32[]{:S(2)}) %collective-permute-start.2) | collective-permute-done | bytes 12320 | tf_op jit(solution)/shard_map/ppermute | solution.py:25
  21.2 3.6 %collective-permute-start.5 = (f32[3,1,2,512]{3,2,1,0:T(2,128)S(1)}, f32[3,1,2,512]{3,2,1,0:T(2,128)S(1)}, u32[]{:S(2)}, u32[]{:S(2)}) collective-permute-start(f32[3,1,2,512]{3,2,1,0:T(2,128)S(1)} %get-tuple-element.115), channel_id=1, source_target_pairs={{1,0},{2,1},{3,2},{4,3},{5,4},{6,5},{7,6},{0,7},{9,8},{10,9},{11,1... | collective-permute-start | bytes 36872 | tf_op jit(solution)/shard_map/ppermute | solution.py:27
  26.4 1.9 %collective-permute-start.10 = (f32[12,4,10,1]{3,0,2,1:T(8,128)}, f32[12,4,10,1]{3,0,2,1:T(8,128)S(1)}, u32[]{:S(2)}, u32[]{:S(2)}) collective-permute-start(f32[12,4,10,1]{3,0,2,1:T(8,128)} %get-tuple-element.62), channel_id=1, source_target_pairs={{0,8},{8,16},{16,24},{24,0},{1,9},{9,17},{17,25},{25,1},{2,10},{10... | collective-permute-start | bytes 5768 | tf_op jit(solution)/shard_map/ppermute | solution.py:25
  30.1 3.5 %collective-permute-start.7 = (f32[3,1,2,512]{3,2,1,0:T(2,128)S(1)}, f32[3,1,2,512]{3,2,1,0:T(2,128)S(1)}, u32[]{:S(2)}, u32[]{:S(2)}) collective-permute-start(f32[3,1,2,512]{3,2,1,0:T(2,128)S(1)} %get-tuple-element.113), channel_id=1, source_target_pairs={{1,0},{2,1},{3,2},{4,3},{5,4},{6,5},{7,6},{0,7},{9,8},{10,9},{11,1... | collective-permute-start | bytes 36872 | tf_op jit(solution)/shard_map/ppermute | solution.py:27
  37.7 3.3 %reduce = f32[512,3,8]{2,1,0:T(4,128)S(1)} reduce(f32[512,3,1,8]{3,2,1,0:T(1,128)S(1)} %bitcast.196, f32[]{:T(128)} %broadcast.636), dimensions={2}, to_apply=%bitcast.180.reduce_sub_computation | reduce | bytes 98308
  42.3 3.3 %all-to-all-start = ((f32[4,1,3072]{2,1,0:T(1,128)}), f32[4,1,3072]{2,1,0:T(1,128)S(1)}, u32[]{:S(2)}, u32[]{:S(2)}) async-start(f32[4,1,3072]{2,1,0:T(1,128)} %reshape.1268), calls=%async_computation | async-start | bytes 98304 | tf_op jit(solution)/shard_map/all_to_all | solution.py:127
  45.8 4.6 %all-to-all-done = f32[4,1,3072]{2,1,0:T(1,128)S(1)} async-done(((f32[4,1,3072]{2,1,0:T(1,128)}), f32[4,1,3072]{2,1,0:T(1,128)S(1)}, u32[]{:S(2)}, u32[]{:S(2)}) %all-to-all-start) | async-done | bytes 49184 | tf_op jit(solution)/shard_map/all_to_all | solution.py:127
  57.4 2.4 %collective-permute-start.14 = (f32[1,8,128]{2,1,0:T(8,128)S(1)}, f32[1,8,128]{2,1,0:T(8,128)S(1)}, u32[]{:S(2)}, u32[]{:S(2)}) collective-permute-start(f32[1,8,128]{2,1,0:T(8,128)S(1)} %get-tuple-element.228), channel_id=1, source_target_pairs={{0,24},{8,16},{16,8},{24,0},{1,25},{9,17},{17,9},{25,1},{2,26},{10... | collective-permute-start | bytes 12296 | tf_op jit(solution)/shard_map/ppermute | solution.py:169
  60.6 1.3 %collective-permute-done.14 = f32[1,8,128]{2,1,0:T(8,128)S(1)} collective-permute-done((f32[1,8,128]{2,1,0:T(8,128)S(1)}, f32[1,8,128]{2,1,0:T(8,128)S(1)}, u32[]{:S(2)}, u32[]{:S(2)}) %collective-permute-start.14) | collective-permute-done | bytes 4128 | tf_op jit(solution)/shard_map/ppermute | solution.py:169
  62.0 3.5 %collective-permute-start.16 = (f32[3,1,2,512]{3,2,1,0:T(2,128)S(1)}, f32[3,1,2,512]{3,2,1,0:T(2,128)S(1)}, u32[]{:S(2)}, u32[]{:S(2)}) collective-permute-start(f32[3,1,2,512]{3,2,1,0:T(2,128)S(1)} %get-tuple-element.105), channel_id=1, source_target_pairs={{1,0},{2,1},{3,2},{4,3},{5,4},{6,5},{7,6},{0,7},{9,8},{10,9},{11,1... | collective-permute-start | bytes 36872 | tf_op jit(solution)/shard_map/ppermute | solution.py:27
  65.6 3.5 %collective-permute-start.24 = (f32[12,4,1,128]{3,0,2,1:T(8,128)S(1)}, f32[12,4,1,128]{3,0,2,1:T(8,128)S(1)}, u32[]{:S(2)}, u32[]{:S(2)}) collective-permute-start(f32[12,4,1,128]{3,0,2,1:T(8,128)S(1)} %get-tuple-element.65), channel_id=1, source_target_pairs={{1,0},{2,1},{3,2},{4,3},{5,4},{6,5},{7,6},{0,7},{9,8},{10,9},{11,1... | collective-permute-start | bytes 73736 | tf_op jit(solution)/shard_map/ppermute | solution.py:27
  70.1 3.5 %collective-permute-start.18 = (f32[3,1,2,512]{3,2,1,0:T(2,128)S(1)}, f32[3,1,2,512]{3,2,1,0:T(2,128)S(1)}, u32[]{:S(2)}, u32[]{:S(2)}) collective-permute-start(f32[3,1,2,512]{3,2,1,0:T(2,128)S(1)} %get-tuple-element.103), channel_id=1, source_target_pairs={{1,0},{2,1},{3,2},{4,3},{5,4},{6,5},{7,6},{0,7},{9,8},{10,9},{11,1... | collective-permute-start | bytes 36872 | tf_op jit(solution)/shard_map/ppermute | solution.py:27
  73.7 1.3 %collective-permute-done.17 = f32[3,1,2,512]{3,2,1,0:T(2,128)S(1)} collective-permute-done((f32[3,1,2,512]{3,2,1,0:T(2,128)S(1)}, f32[3,1,2,512]{3,2,1,0:T(2,128)S(1)}, u32[]{:S(2)}, u32[]{:S(2)}) %collective-permute-start.17) | collective-permute-done | bytes 12320 | tf_op jit(solution)/shard_map/ppermute | solution.py:25
  76.0 3.6 %collective-permute-start.20 = (f32[3,1,2,512]{3,2,1,0:T(2,128)S(1)}, f32[3,1,2,512]{3,2,1,0:T(2,128)S(1)}, u32[]{:S(2)}, u32[]{:S(2)}) collective-permute-start(f32[3,1,2,512]{3,2,1,0:T(2,128)S(1)} %get-tuple-element.101), channel_id=1, source_target_pairs={{1,0},{2,1},{3,2},{4,3},{5,4},{6,5},{7,6},{0,7},{9,8},{10,9},{11,1... | collective-permute-start | bytes 36872 | tf_op jit(solution)/shard_map/ppermute | solution.py:27
  81.9 3.7 %collective-permute-start.22 = (f32[3,1,2,512]{3,2,1,0:T(2,128)S(1)}, f32[3,1,2,512]{3,2,1,0:T(2,128)S(1)}, u32[]{:S(2)}, u32[]{:S(2)}) collective-permute-start(f32[3,1,2,512]{3,2,1,0:T(2,128)S(1)} %get-tuple-element.99), channel_id=1, source_target_pairs={{1,0},{2,1},{3,2},{4,3},{5,4},{6,5},{7,6},{0,7},{9,8},{10,9},{11,1... | collective-permute-start | bytes 36872 | tf_op jit(solution)/shard_map/ppermute | solution.py:27
  87.4 1.3 %multiply_bitcast_fusion.2 = (f32[1,1,8,512]{3,2,1,0:T(8,128)S(1)}, f32[1,8,512]{2,1,0:T(8,128)S(1)}, f32[1,8,512]{2,1,0:T(8,128)}, f32[1,8,512]{2,1,0:T(8,128)S(1)}, f32[1,8,512]{2,1,0:T(8,128)}) fusion(f32[]{:T(128)} %bitcast.27, f32[1,8,512]{2,1,0:T(8,128)S(1)} %fusion.106, f32[1,8,512]{2,1,0:T(8,128)S(1)} %fusion.144, f32[1,8,512]{2,1,0:T(8,128)S(1)} %fusion.125, ...), kind=kLoop, calls=%fused_computation.359 | loop fusion | flops 200704 | bytes 393220 | tf_op jit(solution)/shard_map/stack | solution.py:128
  89.6 3.3 %reduce.2 = f32[512,3,8]{2,1,0:T(4,128)S(1)} reduce(f32[512,3,1,8]{3,2,1,0:T(1,128)S(1)} %bitcast.198, f32[]{:T(128)} %broadcast.636), dimensions={2}, to_apply=%bitcast.182.reduce_sub_computation | reduce | bytes 98308
  94.2 3.6 %all-to-all-start.1 = ((f32[4,1,3072]{2,1,0:T(1,128)}), f32[4,1,3072]{2,1,0:T(1,128)S(1)}, u32[]{:S(2)}, u32[]{:S(2)}) async-start(f32[4,1,3072]{2,1,0:T(1,128)} %reshape.1270), calls=%async_computation.1 | async-start | bytes 98304 | tf_op jit(solution)/shard_map/all_to_all | solution.py:127
  98.0 2.1 %collective-permute-start.25 = (f32[12,4,10,1]{3,0,2,1:T(8,128)S(1)}, f32[12,4,10,1]{3,0,2,1:T(8,128)S(1)}, u32[]{:S(2)}, u32[]{:S(2)}) collective-permute-start(f32[12,4,10,1]{3,0,2,1:T(8,128)S(1)} %get-tuple-element.60), channel_id=1, source_target_pairs={{0,8},{8,16},{16,24},{24,0},{1,9},{9,17},{17,25},{25,1},{2,10},{10... | collective-permute-start | bytes 5768 | tf_op jit(solution)/shard_map/ppermute | solution.py:25
  105.8 3.0 %collective-permute-done.25 = f32[12,4,10,1]{3,0,2,1:T(8,128)S(1)} collective-permute-done((f32[12,4,10,1]{3,0,2,1:T(8,128)S(1)}, f32[12,4,10,1]{3,0,2,1:T(8,128)S(1)}, u32[]{:S(2)}, u32[]{:S(2)}) %collective-permute-start.25) | collective-permute-done | bytes 1952 | tf_op jit(solution)/shard_map/ppermute | solution.py:25
  108.8 3.5 %collective-permute-done.26 = f32[12,4,10,1]{3,0,2,1:T(8,128)S(1)} collective-permute-done((f32[12,4,10,1]{3,0,2,1:T(8,128)S(1)}, f32[12,4,10,1]{3,0,2,1:T(8,128)S(1)}, u32[]{:S(2)}, u32[]{:S(2)}) %collective-permute-start.26) | collective-permute-done | bytes 1952 | tf_op jit(solution)/shard_map/ppermute | solution.py:27
  (220 shorter events, 40.0 us)
Async XLA Ops:
  1.5 12.9 %collective-permute-start = (f32[3,1,2,512]{3,2,1,0:T(2,128)S(1)}, f32[3,1,2,512]{3,2,1,0:T(2,128)S(1)}, u32[]{:S(2)}, u32[]{:S(2)}) collective-permute-start(f32[3,1,2,512]{3,2,1,0:T(2,128)S(1)} %get-tuple-element.118), channel_id=1, source_target_pairs={{0,1},{1,2},{2,3},{3,4},{4,5},{5,6},{6,7},{7,0},{8,9},{9,10},{10,1... | collective-permute-start | bytes 36872 | tf_op jit(solution)/shard_map/ppermute | solution.py:25
  2.0 12.4 %collective-permute-start.1 = (f32[3,1,2,512]{3,2,1,0:T(2,128)S(1)}, f32[3,1,2,512]{3,2,1,0:T(2,128)S(1)}, u32[]{:S(2)}, u32[]{:S(2)}) collective-permute-start(f32[3,1,2,512]{3,2,1,0:T(2,128)S(1)} %get-tuple-element.119), channel_id=1, source_target_pairs={{1,0},{2,1},{3,2},{4,3},{5,4},{6,5},{7,6},{0,7},{9,8},{10,9},{11,1... | collective-permute-start | bytes 36872 | tf_op jit(solution)/shard_map/ppermute | solution.py:27
  7.2 17.6 %collective-permute-start.8 = (f32[12,4,1,128]{3,0,2,1:T(8,128)S(1)}, f32[12,4,1,128]{3,0,2,1:T(8,128)S(1)}, u32[]{:S(2)}, u32[]{:S(2)}) collective-permute-start(f32[12,4,1,128]{3,0,2,1:T(8,128)S(1)} %get-tuple-element.66), channel_id=1, source_target_pairs={{0,1},{1,2},{2,3},{3,4},{4,5},{5,6},{6,7},{7,0},{8,9},{9,10},{10,1... | collective-permute-start | bytes 73736 | tf_op jit(solution)/shard_map/ppermute | solution.py:25
  7.2 17.6 %collective-permute-start.9 = (f32[12,4,1,128]{3,0,2,1:T(8,128)S(1)}, f32[12,4,1,128]{3,0,2,1:T(8,128)S(1)}, u32[]{:S(2)}, u32[]{:S(2)}) collective-permute-start(f32[12,4,1,128]{3,0,2,1:T(8,128)S(1)} %get-tuple-element.67), channel_id=1, source_target_pairs={{1,0},{2,1},{3,2},{4,3},{5,4},{6,5},{7,6},{0,7},{9,8},{10,9},{11,1... | collective-permute-start | bytes 73736 | tf_op jit(solution)/shard_map/ppermute | solution.py:27
  15.2 5.0 %collective-permute-start.2 = (f32[3,1,2,512]{3,2,1,0:T(2,128)S(1)}, f32[3,1,2,512]{3,2,1,0:T(2,128)S(1)}, u32[]{:S(2)}, u32[]{:S(2)}) collective-permute-start(f32[3,1,2,512]{3,2,1,0:T(2,128)S(1)} %get-tuple-element.116), channel_id=1, source_target_pairs={{0,1},{1,2},{2,3},{3,4},{4,5},{5,6},{6,7},{7,0},{8,9},{9,10},{10,1... | collective-permute-start | bytes 36872 | tf_op jit(solution)/shard_map/ppermute | solution.py:25
  15.3 4.9 %collective-permute-start.3 = (f32[3,1,2,512]{3,2,1,0:T(2,128)S(1)}, f32[3,1,2,512]{3,2,1,0:T(2,128)S(1)}, u32[]{:S(2)}, u32[]{:S(2)}) collective-permute-start(f32[3,1,2,512]{3,2,1,0:T(2,128)S(1)} %get-tuple-element.117), channel_id=1, source_target_pairs={{1,0},{2,1},{3,2},{4,3},{5,4},{6,5},{7,6},{0,7},{9,8},{10,9},{11,1... | collective-permute-start | bytes 36872 | tf_op jit(solution)/shard_map/ppermute | solution.py:27
  21.1 8.3 %collective-permute-start.4 = (f32[3,1,2,512]{3,2,1,0:T(2,128)S(1)}, f32[3,1,2,512]{3,2,1,0:T(2,128)S(1)}, u32[]{:S(2)}, u32[]{:S(2)}) collective-permute-start(f32[3,1,2,512]{3,2,1,0:T(2,128)S(1)} %get-tuple-element.114), channel_id=1, source_target_pairs={{0,1},{1,2},{2,3},{3,4},{4,5},{5,6},{6,7},{7,0},{8,9},{9,10},{10,1... | collective-permute-start | bytes 36872 | tf_op jit(solution)/shard_map/ppermute | solution.py:25
  21.2 8.2 %collective-permute-start.5 = (f32[3,1,2,512]{3,2,1,0:T(2,128)S(1)}, f32[3,1,2,512]{3,2,1,0:T(2,128)S(1)}, u32[]{:S(2)}, u32[]{:S(2)}) collective-permute-start(f32[3,1,2,512]{3,2,1,0:T(2,128)S(1)} %get-tuple-element.115), channel_id=1, source_target_pairs={{1,0},{2,1},{3,2},{4,3},{5,4},{6,5},{7,6},{0,7},{9,8},{10,9},{11,1... | collective-permute-start | bytes 36872 | tf_op jit(solution)/shard_map/ppermute | solution.py:27
  26.4 26.9 %collective-permute-start.10 = (f32[12,4,10,1]{3,0,2,1:T(8,128)}, f32[12,4,10,1]{3,0,2,1:T(8,128)S(1)}, u32[]{:S(2)}, u32[]{:S(2)}) collective-permute-start(f32[12,4,10,1]{3,0,2,1:T(8,128)} %get-tuple-element.62), channel_id=1, source_target_pairs={{0,8},{8,16},{16,24},{24,0},{1,9},{9,17},{17,25},{25,1},{2,10},{10... | collective-permute-start | bytes 5768 | tf_op jit(solution)/shard_map/ppermute | solution.py:25
  28.4 24.9 %collective-permute-start.11 = (f32[12,4,10,1]{3,0,2,1:T(8,128)S(1)}, f32[12,4,10,1]{3,0,2,1:T(8,128)S(1)}, u32[]{:S(2)}, u32[]{:S(2)}) collective-permute-start(f32[12,4,10,1]{3,0,2,1:T(8,128)S(1)} %get-tuple-element.63), channel_id=1, source_target_pairs={{8,0},{16,8},{24,16},{0,24},{9,1},{17,9},{25,17},{1,25},{10,2},{18... | collective-permute-start | bytes 5768 | tf_op jit(solution)/shard_map/ppermute | solution.py:27
  30.1 5.0 %collective-permute-start.6 = (f32[3,1,2,512]{3,2,1,0:T(2,128)S(1)}, f32[3,1,2,512]{3,2,1,0:T(2,128)S(1)}, u32[]{:S(2)}, u32[]{:S(2)}) collective-permute-start(f32[3,1,2,512]{3,2,1,0:T(2,128)S(1)} %get-tuple-element.112), channel_id=1, source_target_pairs={{0,1},{1,2},{2,3},{3,4},{4,5},{5,6},{6,7},{7,0},{8,9},{9,10},{10,1... | collective-permute-start | bytes 36872 | tf_op jit(solution)/shard_map/ppermute | solution.py:25
  42.3 8.1 %all-to-all-start = ((f32[4,1,3072]{2,1,0:T(1,128)}), f32[4,1,3072]{2,1,0:T(1,128)S(1)}, u32[]{:S(2)}, u32[]{:S(2)}) async-start(f32[4,1,3072]{2,1,0:T(1,128)} %reshape.1268), calls=%async_computation | async-start | bytes 98304 | tf_op jit(solution)/shard_map/all_to_all | solution.py:127
  62.0 7.2 %collective-permute-start.15 = (f32[3,1,2,512]{3,2,1,0:T(2,128)S(1)}, f32[3,1,2,512]{3,2,1,0:T(2,128)S(1)}, u32[]{:S(2)}, u32[]{:S(2)}) collective-permute-start(f32[3,1,2,512]{3,2,1,0:T(2,128)S(1)} %get-tuple-element.104), channel_id=1, source_target_pairs={{0,1},{1,2},{2,3},{3,4},{4,5},{5,6},{6,7},{7,0},{8,9},{9,10},{10,1... | collective-permute-start | bytes 36872 | tf_op jit(solution)/shard_map/ppermute | solution.py:25
  62.0 7.1 %collective-permute-start.16 = (f32[3,1,2,512]{3,2,1,0:T(2,128)S(1)}, f32[3,1,2,512]{3,2,1,0:T(2,128)S(1)}, u32[]{:S(2)}, u32[]{:S(2)}) collective-permute-start(f32[3,1,2,512]{3,2,1,0:T(2,128)S(1)} %get-tuple-element.105), channel_id=1, source_target_pairs={{1,0},{2,1},{3,2},{4,3},{5,4},{6,5},{7,6},{0,7},{9,8},{10,9},{11,1... | collective-permute-start | bytes 36872 | tf_op jit(solution)/shard_map/ppermute | solution.py:27
  65.6 8.1 %collective-permute-start.23 = (f32[12,4,1,128]{3,0,2,1:T(8,128)S(1)}, f32[12,4,1,128]{3,0,2,1:T(8,128)S(1)}, u32[]{:S(2)}, u32[]{:S(2)}) collective-permute-start(f32[12,4,1,128]{3,0,2,1:T(8,128)S(1)} %get-tuple-element.64), channel_id=1, source_target_pairs={{0,1},{1,2},{2,3},{3,4},{4,5},{5,6},{6,7},{7,0},{8,9},{9,10},{10,1... | collective-permute-start | bytes 73736 | tf_op jit(solution)/shard_map/ppermute | solution.py:25
  65.6 8.1 %collective-permute-start.24 = (f32[12,4,1,128]{3,0,2,1:T(8,128)S(1)}, f32[12,4,1,128]{3,0,2,1:T(8,128)S(1)}, u32[]{:S(2)}, u32[]{:S(2)}) collective-permute-start(f32[12,4,1,128]{3,0,2,1:T(8,128)S(1)} %get-tuple-element.65), channel_id=1, source_target_pairs={{1,0},{2,1},{3,2},{4,3},{5,4},{6,5},{7,6},{0,7},{9,8},{10,9},{11,1... | collective-permute-start | bytes 73736 | tf_op jit(solution)/shard_map/ppermute | solution.py:27
  70.0 5.0 %collective-permute-start.17 = (f32[3,1,2,512]{3,2,1,0:T(2,128)S(1)}, f32[3,1,2,512]{3,2,1,0:T(2,128)S(1)}, u32[]{:S(2)}, u32[]{:S(2)}) collective-permute-start(f32[3,1,2,512]{3,2,1,0:T(2,128)S(1)} %get-tuple-element.102), channel_id=1, source_target_pairs={{0,1},{1,2},{2,3},{3,4},{4,5},{5,6},{6,7},{7,0},{8,9},{9,10},{10,1... | collective-permute-start | bytes 36872 | tf_op jit(solution)/shard_map/ppermute | solution.py:25
  75.9 5.0 %collective-permute-start.19 = (f32[3,1,2,512]{3,2,1,0:T(2,128)S(1)}, f32[3,1,2,512]{3,2,1,0:T(2,128)S(1)}, u32[]{:S(2)}, u32[]{:S(2)}) collective-permute-start(f32[3,1,2,512]{3,2,1,0:T(2,128)S(1)} %get-tuple-element.100), channel_id=1, source_target_pairs={{0,1},{1,2},{2,3},{3,4},{4,5},{5,6},{6,7},{7,0},{8,9},{9,10},{10,1... | collective-permute-start | bytes 36872 | tf_op jit(solution)/shard_map/ppermute | solution.py:25
  76.0 5.0 %collective-permute-start.20 = (f32[3,1,2,512]{3,2,1,0:T(2,128)S(1)}, f32[3,1,2,512]{3,2,1,0:T(2,128)S(1)}, u32[]{:S(2)}, u32[]{:S(2)}) collective-permute-start(f32[3,1,2,512]{3,2,1,0:T(2,128)S(1)} %get-tuple-element.101), channel_id=1, source_target_pairs={{1,0},{2,1},{3,2},{4,3},{5,4},{6,5},{7,6},{0,7},{9,8},{10,9},{11,1... | collective-permute-start | bytes 36872 | tf_op jit(solution)/shard_map/ppermute | solution.py:27
  81.8 5.0 %collective-permute-start.21 = (f32[3,1,2,512]{3,2,1,0:T(2,128)S(1)}, f32[3,1,2,512]{3,2,1,0:T(2,128)S(1)}, u32[]{:S(2)}, u32[]{:S(2)}) collective-permute-start(f32[3,1,2,512]{3,2,1,0:T(2,128)S(1)} %get-tuple-element.98), channel_id=1, source_target_pairs={{0,1},{1,2},{2,3},{3,4},{4,5},{5,6},{6,7},{7,0},{8,9},{9,10},{10,1... | collective-permute-start | bytes 36872 | tf_op jit(solution)/shard_map/ppermute | solution.py:25
  81.9 5.2 %collective-permute-start.22 = (f32[3,1,2,512]{3,2,1,0:T(2,128)S(1)}, f32[3,1,2,512]{3,2,1,0:T(2,128)S(1)}, u32[]{:S(2)}, u32[]{:S(2)}) collective-permute-start(f32[3,1,2,512]{3,2,1,0:T(2,128)S(1)} %get-tuple-element.99), channel_id=1, source_target_pairs={{1,0},{2,1},{3,2},{4,3},{5,4},{6,5},{7,6},{0,7},{9,8},{10,9},{11,1... | collective-permute-start | bytes 36872 | tf_op jit(solution)/shard_map/ppermute | solution.py:27
  94.2 8.6 %all-to-all-start.1 = ((f32[4,1,3072]{2,1,0:T(1,128)}), f32[4,1,3072]{2,1,0:T(1,128)S(1)}, u32[]{:S(2)}, u32[]{:S(2)}) async-start(f32[4,1,3072]{2,1,0:T(1,128)} %reshape.1270), calls=%async_computation.1 | async-start | bytes 98304 | tf_op jit(solution)/shard_map/all_to_all | solution.py:127
  98.0 10.7 %collective-permute-start.25 = (f32[12,4,10,1]{3,0,2,1:T(8,128)S(1)}, f32[12,4,10,1]{3,0,2,1:T(8,128)S(1)}, u32[]{:S(2)}, u32[]{:S(2)}) collective-permute-start(f32[12,4,10,1]{3,0,2,1:T(8,128)S(1)} %get-tuple-element.60), channel_id=1, source_target_pairs={{0,8},{8,16},{16,24},{24,0},{1,9},{9,17},{17,25},{25,1},{2,10},{10... | collective-permute-start | bytes 5768 | tf_op jit(solution)/shard_map/ppermute | solution.py:25
  100.1 12.2 %collective-permute-start.26 = (f32[12,4,10,1]{3,0,2,1:T(8,128)S(1)}, f32[12,4,10,1]{3,0,2,1:T(8,128)S(1)}, u32[]{:S(2)}, u32[]{:S(2)}) collective-permute-start(f32[12,4,10,1]{3,0,2,1:T(8,128)S(1)} %get-tuple-element.61), channel_id=1, source_target_pairs={{8,0},{16,8},{24,16},{0,24},{9,1},{17,9},{25,17},{1,25},{10,2},{18... | collective-permute-start | bytes 5768 | tf_op jit(solution)/shard_map/ppermute | solution.py:27
  (17 other events, 89.7 us)
